TPU v7x, 128 devices: a whole 4x4x4 slice. The times are simulated.
128 devices in a mesh: grp: 8 (over y, z_hi), seq: 16 (over x, z_lo, core).
Axes of the slice: x: 4, y: 4, z: 4 (z_hi: 2, z_lo: 2; z = z_hi * 2 + z_lo), core: 2. Of those that a mesh axis runs over, the one named last changes fastest.
Arguments:
- queries: bfloat16 [8, 2048, 2048], P('grp', 'seq'), may hold values from -6 to 6
- keys: bfloat16 [8, 2048, 512], P('grp', 'seq'), may hold values from -6 to 6
- values: bfloat16 [8, 2048, 512], P('grp', 'seq'), may hold values from -6 to 6
- route_ids: int32 [8, 2048, 8], P('grp', 'seq'), may hold values from 0 to 127, all different within a row; in each aligned block of 128 rows (0 to 127, 128 to 255, ..., all dimensions but the last counted through in order) at most 9 rows name the same one
- route_weights: float32 [8, 2048, 8], P('grp', 'seq'), may hold values from 0.05 to 0.3
- out_weight: bfloat16 [2048, 2048], replicated, may hold values from -1.5909903 to 1.5909903
- norm_gain: float32 [2048], replicated, may hold values from 0.5 to 1.5
- gate_up: bfloat16 [128, 2048, 1536], P(('grp', 'seq')), may hold values from -0.125 to 0.125
- down_weight: bfloat16 [128, 768, 2048], P(('grp', 'seq')), may hold values from -0.21875 to 0.21875
Outputs:
- mixed: bfloat16 [8, 2048, 2048], P('grp', 'seq')
Inputs may be any that keep to these rules, and one draw needn't show every extreme that they name: `route_ids`: each row names 8 different experts; the rows of one device name no expert more than 9 times, and in some devices' rows some expert exactly 9 times.
All inputs are finite; a program needn't handle non-finite values.
Results may differ from a plain program's by a relative error of at most 0.008.
Values may be sent and summed in bfloat16 or wider, within the bound.
No kernel may reach another device: no remote copies, remote signals or barrier semaphores. Data moves between devices by JAX's collectives and lax.ppermute only.
A program may use at most 128 MiB of HBM per device.

v0:
```python
import functools

import jax
import jax.numpy as jnp
from jax import lax
from jax.experimental import pallas as pl
from jax.experimental.pallas import tpu as pltpu
from jax.sharding import PartitionSpec as P


BF16, F32 = jnp.bfloat16, jnp.float32
D = 2048
HEAD = 128
FF = 768
TOP = 8
ROWS = 8
FOLD = D // ROWS
WIDE = D + FOLD
EXPERTS = 128
TOK = 128
VMEM = pl.BlockSpec(memory_space=pltpu.VMEM)


def dot(a, b, dims=((1,), (0,))):
    return lax.dot_general(a, b, (dims, ((), ())), preferred_element_type=F32)


def iota(shape, dim):
    return lax.broadcasted_iota(jnp.int32, shape, dim)


def call(kernel, out, scratch=(), limit=20 << 20, cost=None, **spec):
    return pl.pallas_call(
        kernel,
        out_shape=out,
        scratch_shapes=scratch,
        compiler_params=pltpu.CompilerParams(vmem_limit_bytes=limit),
        cost_estimate=cost,
        **spec,
    )


def pack_kernel(parts, shared, q_far, k_far, v_far, *refs):
    outs, (q_ref, k_ref, v_ref, sems) = refs[: 2 * parts], refs[2 * parts :]
    loads = [
        pltpu.make_async_copy(far, near, sems.at[n])
        for n, (far, near) in enumerate(((k_far, k_ref), (v_far, v_ref), (q_far, q_ref)))
    ]
    for load in loads:
        load.start()
    mine = lax.axis_index("seq") // parts
    for load in loads:
        load.wait()
    for s in range(parts):
        g = lax.rem(mine + s, parts)
        kv_ref, query_ref = outs[s], outs[parts + s]
        lane = pl.multiple_of(g * HEAD, HEAD)
        kv_ref[:TOK, :] = k_ref[:, pl.ds(lane, HEAD)]
        kv_ref[TOK:, :] = v_ref[:, pl.ds(lane, HEAD)]
        for h in range(shared):
            lane = pl.multiple_of(g * (shared * HEAD), HEAD) + h * HEAD
            query_ref[h * TOK : (h + 1) * TOK, :] = q_ref[:, pl.ds(lane, HEAD)]


def join_kernel(parts, *refs):
    mine = lax.axis_index("seq") // parts
    for s in range(parts):
        at = pl.multiple_of(lax.rem(mine - s + parts, parts) * (2 * TOK), 2 * TOK)
        refs[parts][pl.ds(at, 2 * TOK), :] = refs[s][...]


def attention_kernel(parts, shared, *refs):
    kvs, queries, w_ref = refs[:4], refs[4 : 4 + parts], refs[4 + parts]
    outs, near_ref = refs[5 + parts : 5 + 2 * parts], refs[5 + 2 * parts]
    k_s, v_s, q_s, o_s, sem = refs[6 + 2 * parts :]
    carry = pltpu.make_async_copy(w_ref, near_ref, sem)
    carry.start()
    me = lax.axis_index("seq")
    mine, lane_id = me // parts, lax.rem(me, parts)
    rows, keys = shared * TOK, 4 * TOK
    for d in range(4):
        for p in range(parts):
            at = pl.multiple_of((p * 4 + (lane_id ^ d)) * TOK, TOK)
            k_s[pl.ds(at, TOK), :] = kvs[d][p * 2 * TOK : (p * 2 + 1) * TOK, :]
            v_s[pl.ds(at, TOK), :] = kvs[d][(p * 2 + 1) * TOK : (p * 2 + 2) * TOK, :]
    for s in range(parts):
        at = pl.multiple_of(lax.rem(mine - s + parts, parts) * rows, rows)
        q_s[pl.ds(at, rows), :] = queries[s][...]
    factor = HEAD ** (-0.5) * 1.4426950408889634
    keep = iota((rows, keys), 1) <= iota((rows, keys), 0) % TOK + lane_id * TOK
    for i in range(parts):
        q = q_s[i * rows : (i + 1) * rows, :]
        own = dot(q, k_s[i * keys : (i + 1) * keys, :], ((1,), (1,)))
        own = jnp.where(keep, own, -jnp.inf)
        top = jnp.max(own, axis=-1, keepdims=True)
        if i:
            past = dot(q, k_s[: i * keys, :], ((1,), (1,)))
            top = jnp.maximum(top, jnp.max(past, axis=-1, keepdims=True))
            past = jnp.exp2((past - top) * factor)
        own = jnp.exp2((own - top) * factor)
        total = jnp.sum(own, axis=-1, keepdims=True)
        if i:
            total += jnp.sum(past, axis=-1, keepdims=True)
        share = 1.0 / total
        out = dot((own * share).astype(BF16), v_s[i * keys : (i + 1) * keys, :])
        if i:
            out += dot((past * share).astype(BF16), v_s[: i * keys, :])
        o_s[i * rows : (i + 1) * rows, :] = out.astype(BF16)
    for s in range(parts):
        at = pl.multiple_of(lax.rem(mine + s, parts) * rows, rows)
        outs[s][...] = o_s[pl.ds(at, rows), :]
    carry.wait()


def named(ids):
    experts = iota((EXPERTS, TOK), 0)
    return [ids[j : j + 1, :] == experts for j in range(TOP)]


def places(ids):
    hit = jnp.zeros((EXPERTS, TOK), F32)
    for match in named(ids):
        hit += jnp.where(match, 1.0, 0.0)
    before = jnp.where(iota((TOK, TOK), 0) < iota((TOK, TOK), 1), 1.0, 0.0).astype(BF16)
    return jnp.where(hit > 0.5, dot(hit.astype(BF16), before), -1.0)


def spread(rows):
    n, t = rows.shape
    return jnp.broadcast_to(rows[:, None, :], (n, ROWS, t)).reshape(n * ROWS, t)


def put_fold(fold_s, c, value):
    for half in range(FOLD // HEAD):
        fold_s[half, pl.ds(c, value.shape[0], stride=ROWS), :] = value[:, half * HEAD : (half + 1) * HEAD]


def take_fold(fold_s, c, count):
    halves = [fold_s[half, pl.ds(c, count, stride=ROWS), :] for half in range(FOLD // HEAD)]
    return jnp.concatenate(halves, axis=1).astype(BF16)


def load_fold(fold_s, tail):
    for half in range(FOLD // HEAD):
        fold_s[half] = tail[:, half * HEAD : (half + 1) * HEAD].astype(F32)


def whole_fold(fold_s):
    return jnp.concatenate([fold_s[half] for half in range(FOLD // HEAD)], axis=1).astype(BF16)


def project_kernel(parts, shared, *refs):
    pieces = refs[:parts]
    w_ref, gain_ref, ids_ref, hidden_ref, o_ref, normed_s, fold_s = refs[parts:]
    mine = lax.axis_index("seq") // parts
    wide, rows = shared * HEAD, TOK
    power = jnp.zeros((rows, 1), F32)
    step = 512
    for c in range(0, D, step):
        h = jnp.zeros((rows, step), F32)
        for s in range(parts):
            a = jnp.concatenate([pieces[s][g * rows : (g + 1) * rows, :] for g in range(shared)], axis=1)
            at = pl.multiple_of(lax.rem(mine - s + parts, parts) * wide, wide)
            h += dot(a, w_ref[pl.ds(at, wide), c : c + step])
        hidden_ref[:, c : c + step] = h
        power += jnp.sum(h * h, axis=-1, keepdims=True)
    scale = lax.rsqrt(power * (1.0 / D) + 1e-06)
    for c in range(0, D, step):
        normed_s[:, c : c + step] = (
            hidden_ref[:, c : c + step] * scale * gain_ref[:, c : c + step]
        ).astype(BF16)
    place = places(ids_ref[...])
    wide = spread(place)
    which = iota((EXPERTS * ROWS, TOK), 0) % ROWS
    pick = jnp.where(wide == which.astype(F32), 1.0, 0.0).astype(BF16)
    ninth = jnp.where(place == float(ROWS), 1.0, 0.0).astype(BF16)
    for c in range(ROWS):
        piece = normed_s[:, c * FOLD : (c + 1) * FOLD]
        o_ref[:, c * FOLD : (c + 1) * FOLD] = dot(pick, piece).astype(BF16)
        put_fold(fold_s, c, dot(ninth, piece))
    o_ref[:, D:] = whole_fold(fold_s)


def expert_kernel(count, x_ref, wide_ref, down_ref, o_ref, last_s, fold_s):
    def mlp(x):
        gate = dot(x, wide_ref[:, :FF])
        up = dot(x, wide_ref[:, FF:])
        inner = (gate / (1.0 + jnp.exp(-gate)) * up).astype(BF16)
        return dot(inner, down_ref[...])

    block = 256
    for b in range(0, count * ROWS, block):
        o_ref[b : b + block, :D] = mlp(x_ref[b : b + block, :D]).astype(BF16)
    load_fold(fold_s, x_ref[:, D:])
    for c in range(ROWS):
        last_s[:, c * FOLD : (c + 1) * FOLD] = take_fold(fold_s, c, count)
    last = mlp(last_s[...])
    for c in range(ROWS):
        put_fold(fold_s, c, last[:, c * FOLD : (c + 1) * FOLD])
    o_ref[:, D:] = whole_fold(fold_s)


def share_kernel(ids_ref, weights_ref, share_ref, ninth_ref):
    def halves(value, ref):
        high = value.astype(BF16)
        ref[:TOK, :] = high
        ref[TOK:, :] = (value - high.astype(F32)).astype(BF16)

    ids = ids_ref[...]
    place = places(ids)
    weight = jnp.zeros((EXPERTS, TOK), F32)
    for j, match in enumerate(named(ids)):
        weight += jnp.where(match, weights_ref[j : j + 1, :], 0.0)
    which = (iota((EXPERTS * ROWS, TOK), 0) % ROWS).astype(F32)
    halves(jnp.where(spread(place) == which, spread(weight), 0.0).T, share_ref)
    halves(jnp.where(place == float(ROWS), weight, 0.0).T, ninth_ref)


def combine_kernel(y_ref, share_ref, ninth_ref, hidden_ref, o_ref, fold_s):
    load_fold(fold_s, y_ref[:, D:])
    for c in range(ROWS):
        cols = slice(c * FOLD, (c + 1) * FOLD)
        last = take_fold(fold_s, c, EXPERTS)
        mixture = dot(share_ref[...], y_ref[:, cols]) + dot(ninth_ref[...], last)
        o_ref[:, cols] = (hidden_ref[:, cols] + mixture[:TOK] + mixture[TOK:]).astype(BF16)


def exchange(value, axes):
    return lax.all_to_all(value, axes, split_axis=0, concat_axis=0, tiled=True)


def shaped(*dims, dtype=BF16):
    return jax.ShapeDtypeStruct(dims, dtype)


def on_device(
    queries, keys, values, route_ids, route_weights, out_weight, norm_gain, gate_up, down_weight
):
    heads, parts = queries.shape[2] // HEAD, keys.shape[2] // HEAD
    shared = heads // parts
    size = lax.axis_size("seq")
    ids = route_ids[0].T

    def ahead(value, s):
        return lax.ppermute(value, "seq", [(i, (i + s * parts) % size) for i in range(size)])

    def across(value, d):
        return lax.ppermute(value, "seq", [(i, i ^ d) for i in range(size)])

    kv, query = shaped(2 * TOK, HEAD), shaped(shared * TOK, HEAD)
    sent = call(
        functools.partial(pack_kernel, parts, shared),
        (kv,) * parts + (query,) * parts,
        [pltpu.VMEM(a.shape[1:], BF16) for a in (queries, keys, values)] + [pltpu.SemaphoreType.DMA((3,))],
        limit=107 << 19,
        in_specs=[pl.BlockSpec(memory_space=pltpu.HBM)] * 3,
    )(queries[0], keys[0], values[0])
    kvs = [sent[0]] + [ahead(sent[s], s) for s in range(1, parts)]
    asked = [sent[parts]] + [ahead(sent[parts + s], s) for s in range(1, parts)]
    line = call(functools.partial(join_kernel, parts), shaped(parts * 2 * TOK, HEAD))(*kvs)
    flipped = across(line, 2)
    gathered = [line, across(line, 1), flipped, across(flipped, 1)]
    share, ninth = call(
        share_kernel, (shaped(2 * TOK, EXPERTS * ROWS), shaped(2 * TOK, EXPERTS))
    )(ids, route_weights[0].T)
    gathered, share, ninth = lax.optimization_barrier((gathered, share, ninth))
    *attended, weight = call(
        functools.partial(attention_kernel, parts, shared),
        (query,) * parts + (shaped(*out_weight.shape),),
        [pltpu.VMEM((size * TOK, HEAD), BF16)] * 2
        + [pltpu.VMEM((parts * shared * TOK, HEAD), BF16)] * 2
        + [pltpu.SemaphoreType.DMA],
        limit=40 << 20,
        in_specs=[VMEM] * (4 + parts) + [pl.BlockSpec(memory_space=pltpu.HBM)],
        out_specs=(VMEM,) * (parts + 1),
    )(*gathered, *asked, out_weight)
    attended = [attended[0]] + [ahead(attended[s], s) for s in range(1, parts)]
    hidden, outgoing = call(
        functools.partial(project_kernel, parts, shared),
        (shaped(TOK, D, dtype=F32), shaped(EXPERTS * ROWS, WIDE)),
        [pltpu.VMEM((TOK, D), BF16), pltpu.VMEM((FOLD // HEAD, EXPERTS * ROWS, HEAD), F32)],
    )(*attended, weight, norm_gain[None], ids)
    arrived = exchange(outgoing, ("grp", "seq"))
    fold = pltpu.VMEM((FOLD // HEAD, EXPERTS * ROWS, HEAD), F32)
    result = call(
        functools.partial(expert_kernel, EXPERTS),
        shaped(EXPERTS * ROWS, WIDE),
        [pltpu.VMEM((EXPERTS, D), BF16), fold],
    )(arrived, gate_up[0], down_weight[0])
    returned = exchange(result, ("grp", "seq"))
    mixed = call(combine_kernel, shaped(TOK, D), [fold])(returned, share, ninth, hidden)
    return mixed[None]


def solution(mesh):
    placed = (
        P("grp", "seq", None),
        P("grp", "seq", None),
        P("grp", "seq", None),
        P("grp", "seq", None),
        P("grp", "seq", None),
        P(),
        P(),
        P(("grp", "seq"), None, None),
        P(("grp", "seq"), None, None),
    )

    return jax.shard_map(on_device, mesh=mesh, in_specs=placed, out_specs=P("grp", "seq", None), check_vma=False)
```

profile of v0, /device:TPU:4, one launch (start us, length us, event | category | flops | bytes accessed | tf_op | source)
XLA Modules:
  0.0 192.6 jit_solution(1540783803782818511)
XLA Ops:
  0.0 2.1 %shard_map.91 = (bf16[256,128]{1,0:T(8,128)(2,1)S(1)}, bf16[256,128]{1,0:T(8,128)(2,1)S(1)}, bf16[256,128]{1,0:T(8,128)(2,1)S(1)}, bf16[256,128]{1,0:T(8,128)(2,...) custom-call(bf16[128,2048]{1,0:T(8,128)(2,1)} %bitcast.29, ...), custom_call_target="tpu_custom_call" | custom-call | tf_op jit(solution)/shard_map/pallas_call | solution.py:251
  2.1 1.3 collective-permute-start
  3.4 0.8 collective-permute-start.1
  4.1 1.0 collective-permute-start.2
  5.2 1.2 collective-permute-done.refs_1_
  6.4 2.7 %collective-permute-done.1.refs_2_ = bf16[256,128]{1,0:T(8,128)(2,1)S(1)} collective-permute-done((bf16[256,128]{1,0:T(8,128)(2,1)S(1)}, bf16[256,128]{1,0:T(8,128)(2,1)S(1)}, u32[]{:S(2)}, u32[]{:S(2)}) %collective-permute-start.1) | collective-permute-done | bytes 65568 | tf_op jit(solution)/shard_map/ppermute | solution.py:245
  9.1 0.1 collective-permute-done.2.refs_3_
  9.2 2.0 %collective-permute-start.4 = (bf16[1024,128]{1,0:T(8,128)(2,1)S(1)}, bf16[1024,128]{1,0:T(8,128)(2,1)S(1)}, u32[]{:S(2)}, u32[]{:S(2)}) collective-permute-start(bf16[1024,128]{1,0:T(8,128)(2,1)S(1)} %shard_map.92.refs_0_), channel_id=1, source_target_pairs={{0,2},{1,3},{2,0},{3,1},{4,6},{5,7},{6,4},{7,5},{8,10},{9,11},{10,... | collective-permute-start | bytes 786440 | tf_op jit(solution)/shard_map/ppermute | solution.py:248
  11.2 0.0 collective-permute-start.3
  11.2 4.9 %collective-permute-done.4.refs_2_ = bf16[1024,128]{1,0:T(8,128)(2,1)S(1)} collective-permute-done((bf16[1024,128]{1,0:T(8,128)(2,1)S(1)}, bf16[1024,128]{1,0:T(8,128)(2,1)S(1)}, u32[]{:S(2)}, u32[]{:S(2)}) %collective-permute-start.4) | collective-permute-done | bytes 262176 | tf_op jit(solution)/shard_map/ppermute | solution.py:248
  16.1 0.0 collective-permute-start.5
  16.1 2.5 %collective-permute-start.6 = (bf16[512,128]{1,0:T(8,128)(2,1)}, bf16[512,128]{1,0:T(8,128)(2,1)S(1)}, u32[]{:S(2)}, u32[]{:S(2)}) collective-permute-start(bf16[512,128]{1,0:T(8,128)(2,1)} %get-tuple-element.39), channel_id=1, source_target_pairs={{0,4},{1,5},{2,6},{3,7},{4,8},{5,9},{6,10},{7,11},{8,12},{9,13},{1... | collective-permute-start | bytes 393224 | tf_op jit(solution)/shard_map/ppermute | solution.py:245
  18.6 0.0 collective-permute-start.7
  18.6 2.3 %collective-permute-start.8 = (bf16[512,128]{1,0:T(8,128)(2,1)}, bf16[512,128]{1,0:T(8,128)(2,1)S(1)}, u32[]{:S(2)}, u32[]{:S(2)}) collective-permute-start(bf16[512,128]{1,0:T(8,128)(2,1)} %get-tuple-element.41), channel_id=1, source_target_pairs={{0,12},{1,13},{2,14},{3,15},{4,0},{5,1},{6,2},{7,3},{8,4},{9,5},{1... | collective-permute-start | bytes 393224 | tf_op jit(solution)/shard_map/ppermute | solution.py:245
  21.0 0.0 copy-start.1
  21.0 0.7 copy-done.1
  21.6 0.0 copy-start.4
  21.6 0.7 copy-done.4
  22.3 0.4 shard_map.93
  22.8 0.0 collective-permute-done.3.refs_1_
  22.8 0.0 collective-permute-done.5.refs_3_
  22.8 0.1 collective-permute-done.6.refs_5_
  22.8 3.1 %collective-permute-done.7.refs_6_ = bf16[512,128]{1,0:T(8,128)(2,1)S(1)} collective-permute-done((bf16[512,128]{1,0:T(8,128)(2,1)}, bf16[512,128]{1,0:T(8,128)(2,1)S(1)}, u32[]{:S(2)}, u32[]{:S(2)}) %collective-permute-start.7) | collective-permute-done | bytes 131104 | tf_op jit(solution)/shard_map/ppermute | solution.py:245
  26.0 0.8 collective-permute-done.8.refs_7_
  26.8 0.0 copy-start.2
  26.8 0.0 copy-start.3
  26.8 5.9 %shard_map.94 = (bf16[512,128]{1,0:T(8,128)(2,1)S(1)}, bf16[512,128]{1,0:T(8,128)(2,1)S(1)}, bf16[512,128]{1,0:T(8,128)(2,1)S(1)}, bf16[512,128]{1,0:T(8,128)(2,1)S(1)}, bf16[2048,2048]{1,0:T(8,128)(2,1)S(1)}) custom-call(bf16[1024,128]{1,0:T(8,128)(2,1)S(1)} %shard_map.92.refs_0_, bf16[1024,128]{1,0:T(8,128)(2,1)S(1)} %collective-permute-done.3.refs_1_, ...), custom_call_target="tpu_custom_call" | custom-call | tf_op jit(solution)/shard_map/pallas_call | solution.py:267
  32.8 2.9 %collective-permute-start.9 = (bf16[512,128]{1,0:T(8,128)(2,1)S(1)}, bf16[512,128]{1,0:T(8,128)(2,1)S(1)}, u32[]{:S(2)}, u32[]{:S(2)}) collective-permute-start(bf16[512,128]{1,0:T(8,128)(2,1)S(1)} %get-tuple-element.43), channel_id=1, source_target_pairs={{0,4},{1,5},{2,6},{3,7},{4,8},{5,9},{6,10},{7,11},{8,12},{9,13},{1... | collective-permute-start | bytes 393224 | tf_op jit(solution)/shard_map/ppermute | solution.py:245
  35.7 0.1 collective-permute-start.10
  35.7 1.9 %collective-permute-start.11 = (bf16[512,128]{1,0:T(8,128)(2,1)S(1)}, bf16[512,128]{1,0:T(8,128)(2,1)S(1)}, u32[]{:S(2)}, u32[]{:S(2)}) collective-permute-start(bf16[512,128]{1,0:T(8,128)(2,1)S(1)} %get-tuple-element.45), channel_id=1, source_target_pairs={{0,12},{1,13},{2,14},{3,15},{4,0},{5,1},{6,2},{7,3},{8,4},{9,5},{1... | collective-permute-start | bytes 393224 | tf_op jit(solution)/shard_map/ppermute | solution.py:245
  37.7 1.9 collective-permute-done.9.refs_1_
  39.5 2.8 %collective-permute-done.10.refs_2_ = bf16[512,128]{1,0:T(8,128)(2,1)S(1)} collective-permute-done((bf16[512,128]{1,0:T(8,128)(2,1)S(1)}, bf16[512,128]{1,0:T(8,128)(2,1)S(1)}, u32[]{:S(2)}, u32[]{:S(2)}) %collective-permute-start.10) | collective-permute-done | bytes 131104 | tf_op jit(solution)/shard_map/ppermute | solution.py:245
  42.3 0.3 collective-permute-done.11.refs_3_
  42.6 0.0 copy-done.2
  42.6 0.0 copy-done.3
  42.6 0.0 slice-start
  42.6 2.9 %shard_map.95 = (f32[128,2048]{1,0:T(8,128)S(1)}, bf16[1024,2304]{1,0:T(8,128)(2,1)S(1)}) custom-call(bf16[512,128]{1,0:T(8,128)(2,1)S(1)} %get-tuple-element.42.refs_0_, bf16[512,128]{1,0:T(8,128)(2,1)S(1)} %collective-permute-done.9.refs_1_, bf16[512,128]{1,0:T(8,128)(2,1)S(1)} %collective-permute-done.10.refs_2_, ...), custom_call_target="tpu_custom_call" | custom-call | tf_op jit(solution)/shard_map/pallas_call | solution.py:278
  45.5 0.0 slice-start.1
  45.5 0.0 copy-start
  45.5 69.9 %all_to_all.22 = bf16[128,8,2304]{2,1,0:T(8,128)(2,1)S(1)} all-to-all(bf16[128,8,2304]{2,1,0:T(8,128)(2,1)S(1)} %bitcast.23), channel_id=1, replica_groups=mesh['grp'=8,'seq'=16] {'grp','seq'}, dimensions={0} | all-to-all | bytes 9437184 | tf_op jit(solution)/shard_map/all_to_all | solution.py:229
  115.5 0.0 slice-done
  115.5 0.0 slice-done.1
  115.5 0.0 copy-done
  115.5 11.3 %shard_map.96 = bf16[1024,2304]{1,0:T(8,128)(2,1)S(1)} custom-call(bf16[1024,2304]{1,0:T(8,128)(2,1)S(1)} %bitcast.18, bf16[2048,1536]{1,0:T(8,128)(2,1)S(1)} %bitcast.22, bf16[768,2048]{1,0:T(8,128)(2,1)S(1)} %bitcast.24), custom_call_target="tpu_custom_call" | custom-call | tf_op jit(solution)/shard_map/pallas_call | solution.py:285
  126.9 63.3 %all_to_all.23 = bf16[128,8,2304]{2,1,0:T(8,128)(2,1)S(1)} all-to-all(bf16[128,8,2304]{2,1,0:T(8,128)(2,1)S(1)} %bitcast.19), channel_id=1, replica_groups=mesh['grp'=8,'seq'=16] {'grp','seq'}, dimensions={0} | all-to-all | bytes 9437184 | tf_op jit(solution)/shard_map/all_to_all | solution.py:229
  190.2 2.4 %shard_map.97 = bf16[128,2048]{1,0:T(8,128)(2,1)} custom-call(bf16[1024,2304]{1,0:T(8,128)(2,1)S(1)} %bitcast.17, bf16[256,1024]{1,0:T(8,128)(2,1)S(1)} %get-tuple-element.48.share_ref, bf16[256,128]{1,0:T(8,128)(2,1)S(1)} %get-tuple-element.49.ninth_ref, f32[128,2048]{1,0:T(8,128)S(1)} %get-tuple-element.50.hidden_ref), custom_call_target="tpu_custom_call" | custom-call | tf_op jit(solution)/shard_map/pallas_call | solution.py:291
  (2 shorter events, 0.0 us)
Async XLA Ops:
  2.1 4.3 %collective-permute-start = (bf16[256,128]{1,0:T(8,128)(2,1)S(1)}, bf16[256,128]{1,0:T(8,128)(2,1)S(1)}, u32[]{:S(2)}, u32[]{:S(2)}) collective-permute-start(bf16[256,128]{1,0:T(8,128)(2,1)S(1)} %get-tuple-element.29), channel_id=1, source_target_pairs={{0,4},{1,5},{2,6},{3,7},{4,8},{5,9},{6,10},{7,11},{8,12},{9,13},{1... | collective-permute-start | bytes 196616 | tf_op jit(solution)/shard_map/ppermute | solution.py:245
  3.4 5.8 %collective-permute-start.1 = (bf16[256,128]{1,0:T(8,128)(2,1)S(1)}, bf16[256,128]{1,0:T(8,128)(2,1)S(1)}, u32[]{:S(2)}, u32[]{:S(2)}) collective-permute-start(bf16[256,128]{1,0:T(8,128)(2,1)S(1)} %get-tuple-element.30), channel_id=1, source_target_pairs={{0,8},{1,9},{2,10},{3,11},{4,12},{5,13},{6,14},{7,15},{8,0},{9,1},... | collective-permute-start | bytes 196616 | tf_op jit(solution)/shard_map/ppermute | solution.py:245
  4.1 5.0 %collective-permute-start.2 = (bf16[256,128]{1,0:T(8,128)(2,1)S(1)}, bf16[256,128]{1,0:T(8,128)(2,1)S(1)}, u32[]{:S(2)}, u32[]{:S(2)}) collective-permute-start(bf16[256,128]{1,0:T(8,128)(2,1)S(1)} %get-tuple-element.31), channel_id=1, source_target_pairs={{0,12},{1,13},{2,14},{3,15},{4,0},{5,1},{6,2},{7,3},{8,4},{9,5},{1... | collective-permute-start | bytes 196616 | tf_op jit(solution)/shard_map/ppermute | solution.py:245
  9.2 6.9 %collective-permute-start.4 = (bf16[1024,128]{1,0:T(8,128)(2,1)S(1)}, bf16[1024,128]{1,0:T(8,128)(2,1)S(1)}, u32[]{:S(2)}, u32[]{:S(2)}) collective-permute-start(bf16[1024,128]{1,0:T(8,128)(2,1)S(1)} %shard_map.92.refs_0_), channel_id=1, source_target_pairs={{0,2},{1,3},{2,0},{3,1},{4,6},{5,7},{6,4},{7,5},{8,10},{9,11},{10,... | collective-permute-start | bytes 786440 | tf_op jit(solution)/shard_map/ppermute | solution.py:248
  11.2 11.5 %collective-permute-start.3 = (bf16[1024,128]{1,0:T(8,128)(2,1)S(1)}, bf16[1024,128]{1,0:T(8,128)(2,1)S(1)}, u32[]{:S(2)}, u32[]{:S(2)}) collective-permute-start(bf16[1024,128]{1,0:T(8,128)(2,1)S(1)} %shard_map.92.refs_0_), channel_id=1, source_target_pairs={{0,1},{1,0},{2,3},{3,2},{4,5},{5,4},{6,7},{7,6},{8,9},{9,8},{10,11... | collective-permute-start | bytes 786440 | tf_op jit(solution)/shard_map/ppermute | solution.py:248
  16.1 6.7 %collective-permute-start.5 = (bf16[1024,128]{1,0:T(8,128)(2,1)S(1)}, bf16[1024,128]{1,0:T(8,128)(2,1)S(1)}, u32[]{:S(2)}, u32[]{:S(2)}) collective-permute-start(bf16[1024,128]{1,0:T(8,128)(2,1)S(1)} %collective-permute-done.4.refs_2_), channel_id=1, source_target_pairs={{0,1},{1,0},{2,3},{3,2},{4,5},{5,4},{6,7},{7,6},{8,9},{9,8},{10,11... | collective-permute-start | bytes 786440 | tf_op jit(solution)/shard_map/ppermute | solution.py:248
  16.1 6.7 %collective-permute-start.6 = (bf16[512,128]{1,0:T(8,128)(2,1)}, bf16[512,128]{1,0:T(8,128)(2,1)S(1)}, u32[]{:S(2)}, u32[]{:S(2)}) collective-permute-start(bf16[512,128]{1,0:T(8,128)(2,1)} %get-tuple-element.39), channel_id=1, source_target_pairs={{0,4},{1,5},{2,6},{3,7},{4,8},{5,9},{6,10},{7,11},{8,12},{9,13},{1... | collective-permute-start | bytes 393224 | tf_op jit(solution)/shard_map/ppermute | solution.py:245
  18.6 7.3 %collective-permute-start.7 = (bf16[512,128]{1,0:T(8,128)(2,1)}, bf16[512,128]{1,0:T(8,128)(2,1)S(1)}, u32[]{:S(2)}, u32[]{:S(2)}) collective-permute-start(bf16[512,128]{1,0:T(8,128)(2,1)} %get-tuple-element.40), channel_id=1, source_target_pairs={{0,8},{1,9},{2,10},{3,11},{4,12},{5,13},{6,14},{7,15},{8,0},{9,1},... | collective-permute-start | bytes 393224 | tf_op jit(solution)/shard_map/ppermute | solution.py:245
  18.6 8.2 %collective-permute-start.8 = (bf16[512,128]{1,0:T(8,128)(2,1)}, bf16[512,128]{1,0:T(8,128)(2,1)S(1)}, u32[]{:S(2)}, u32[]{:S(2)}) collective-permute-start(bf16[512,128]{1,0:T(8,128)(2,1)} %get-tuple-element.41), channel_id=1, source_target_pairs={{0,12},{1,13},{2,14},{3,15},{4,0},{5,1},{6,2},{7,3},{8,4},{9,5},{1... | collective-permute-start | bytes 393224 | tf_op jit(solution)/shard_map/ppermute | solution.py:245
  21.0 0.7 copy-start.1
  21.6 0.7 copy-start.4
  26.8 15.8 %copy-start.2 = (s32[1,128,8]{1,2,0:T(8,128)S(1)}, s32[1,128,8]{1,2,0:T(8,128)}, u32[]{:S(2)}) copy-start(s32[1,128,8]{1,2,0:T(8,128)} %param.12) | copy-start | bytes 12292
  26.8 15.8 %copy-start.3 = (f32[2048]{0:T(1024)S(1)}, f32[2048]{0:T(1024)}, u32[]{:S(2)}) copy-start(f32[2048]{0:T(1024)} %param.15) | copy-start | bytes 24580
  32.8 6.8 %collective-permute-start.9 = (bf16[512,128]{1,0:T(8,128)(2,1)S(1)}, bf16[512,128]{1,0:T(8,128)(2,1)S(1)}, u32[]{:S(2)}, u32[]{:S(2)}) collective-permute-start(bf16[512,128]{1,0:T(8,128)(2,1)S(1)} %get-tuple-element.43), channel_id=1, source_target_pairs={{0,4},{1,5},{2,6},{3,7},{4,8},{5,9},{6,10},{7,11},{8,12},{9,13},{1... | collective-permute-start | bytes 393224 | tf_op jit(solution)/shard_map/ppermute | solution.py:245
  35.7 6.7 %collective-permute-start.10 = (bf16[512,128]{1,0:T(8,128)(2,1)S(1)}, bf16[512,128]{1,0:T(8,128)(2,1)S(1)}, u32[]{:S(2)}, u32[]{:S(2)}) collective-permute-start(bf16[512,128]{1,0:T(8,128)(2,1)S(1)} %get-tuple-element.44), channel_id=1, source_target_pairs={{0,8},{1,9},{2,10},{3,11},{4,12},{5,13},{6,14},{7,15},{8,0},{9,1},... | collective-permute-start | bytes 393224 | tf_op jit(solution)/shard_map/ppermute | solution.py:245
  35.7 6.9 %collective-permute-start.11 = (bf16[512,128]{1,0:T(8,128)(2,1)S(1)}, bf16[512,128]{1,0:T(8,128)(2,1)S(1)}, u32[]{:S(2)}, u32[]{:S(2)}) collective-permute-start(bf16[512,128]{1,0:T(8,128)(2,1)S(1)} %get-tuple-element.45), channel_id=1, source_target_pairs={{0,12},{1,13},{2,14},{3,15},{4,0},{5,1},{6,2},{7,3},{8,4},{9,5},{1... | collective-permute-start | bytes 393224 | tf_op jit(solution)/shard_map/ppermute | solution.py:245
  42.6 72.9 %slice-start = ((s8[6291456]{0:T(1024)(128)(4,1)}), s8[4194304]{0:T(1024)(128)(4,1)S(1)}, s32[]{:S(2)}) async-start(s8[6291456]{0:T(1024)(128)(4,1)} %bitcast.20), calls=%async_computation.2 | async-start | bytes 8388608
  45.5 70.0 %slice-start.1 = ((s8[6291456]{0:T(1024)(128)(4,1)}), s8[2097152]{0:T(1024)(128)(4,1)S(1)}, s32[]{:S(2)}) async-start(s8[6291456]{0:T(1024)(128)(4,1)} %bitcast.20), calls=%async_computation.3 | async-start | bytes 4194304
  45.5 70.0 %copy-start = (bf16[1,768,2048]{2,1,0:T(8,128)(2,1)S(1)}, bf16[1,768,2048]{2,1,0:T(8,128)(2,1)}, u32[]{:S(2)}) copy-start(bf16[1,768,2048]{2,1,0:T(8,128)(2,1)} %param.17) | copy-start | bytes 9437188
where the time goes:
time: 194 us; the launch traced here: 193 us
  blocking collectives  133 us (69%)
  Pallas kernels  25.1 us (13%)
  waiting for transfers between devices  17.9 us (9%)
  starting transfers between devices  14.9 us (8%)
    all_to_all x2, blocking collectives, exchange(): return lax.all_to_all(value, axes, split_axis=0, concat_axis=0, tiled=True)  133 us
    ppermute x9, waiting for transfers between devices, ahead(): lax.ppermute(value, 'seq', [(i, (i + s * parts) % size) for i in range(si...  13 us
    ppermute x9, starting transfers between devices, ahead(): lax.ppermute(value, 'seq', [(i, (i + s * parts) % size) for i in range(si...  12.9 us
    pallas_call x1, Pallas kernels, on_device(): call(functools.partial(expert_kernel, EXPERTS), shaped(EXPERTS * ROWS, WI...  11.3 us
    pallas_call x1, Pallas kernels, on_device(): call(functools.partial(attention_kernel, parts, shared), (query,) * parts...  5.92 us
    ppermute x3, waiting for transfers between devices, across(): return lax.ppermute(value, 'seq', [(i, i ^ d) for i in range(size)])  4.88 us
  transfers between devices with their start and end apart: 12, of which 10 were waited for; matrix products, arithmetic and copies ran while one was open for 0% of the time, Pallas kernels for 0%

commit v1 on v0

--- a/solution.py
+++ b/solution.py
@@ -149,19 +149,52 @@
     return jnp.concatenate([fold_s[half] for half in range(FOLD // HEAD)], axis=1).astype(BF16)
 
 
+def head_rows(piece, shared):
+    return jnp.concatenate([piece[g * TOK : (g + 1) * TOK, :] for g in range(shared)], axis=1)
+
+
+def weight_rows(parts, shared, s):
+    mine = lax.axis_index("seq") // parts
+    wide = shared * HEAD
+    return pl.ds(pl.multiple_of(lax.rem(mine - s + parts, parts) * wide, wide), wide)
+
+
+def prepare_kernel(
+    parts, shared, a_ref, w_ref, ids_ref, weights_ref, part_ref, pick_ref, nine_ref, share_ref, ninth_ref
+):
+    a = head_rows(a_ref, shared)
+    rows = weight_rows(parts, shared, 0)
+    for c in range(0, D, 512):
+        part_ref[:, c : c + 512] = dot(a, w_ref[rows, c : c + 512])
+
+    def halves(value, ref):
+        high = value.astype(BF16)
+        ref[:TOK, :] = high
+        ref[TOK:, :] = (value - high.astype(F32)).astype(BF16)
+
+    ids = ids_ref[...]
+    place = places(ids)
+    weight = jnp.zeros((EXPERTS, TOK), F32)
+    for j, match in enumerate(named(ids)):
+        weight += jnp.where(match, weights_ref[j : j + 1, :], 0.0)
+    which = (iota((EXPERTS * ROWS, TOK), 0) % ROWS).astype(F32)
+    here = spread(place) == which
+    pick_ref[...] = jnp.where(here, 1.0, 0.0).astype(BF16)
+    halves(jnp.where(here, spread(weight), 0.0).T, share_ref)
+    last = place == float(ROWS)
+    nine_ref[...] = jnp.where(last, 1.0, 0.0).astype(BF16)
+    halves(jnp.where(last, weight, 0.0).T, ninth_ref)
+
+
 def project_kernel(parts, shared, *refs):
-    pieces = refs[:parts]
-    w_ref, gain_ref, ids_ref, hidden_ref, o_ref, normed_s, fold_s = refs[parts:]
-    mine = lax.axis_index("seq") // parts
-    wide, rows = shared * HEAD, TOK
-    power = jnp.zeros((rows, 1), F32)
+    pieces = refs[: parts - 1]
+    part_ref, w_ref, gain_ref, pick_ref, nine_ref, hidden_ref, o_ref, normed_s, fold_s = refs[parts - 1 :]
+    power = jnp.zeros((TOK, 1), F32)
     step = 512
     for c in range(0, D, step):
-        h = jnp.zeros((rows, step), F32)
-        for s in range(parts):
-            a = jnp.concatenate([pieces[s][g * rows : (g + 1) * rows, :] for g in range(shared)], axis=1)
-            at = pl.multiple_of(lax.rem(mine - s + parts, parts) * wide, wide)
-            h += dot(a, w_ref[pl.ds(at, wide), c : c + step])
+        h = part_ref[:, c : c + step]
+        for s in range(1, parts):
+            h += dot(head_rows(pieces[s - 1], shared), w_ref[weight_rows(parts, shared, s), c : c + step])
         hidden_ref[:, c : c + step] = h
         power += jnp.sum(h * h, axis=-1, keepdims=True)
     scale = lax.rsqrt(power * (1.0 / D) + 1e-06)
@@ -169,15 +202,10 @@
         normed_s[:, c : c + step] = (
             hidden_ref[:, c : c + step] * scale * gain_ref[:, c : c + step]
         ).astype(BF16)
-    place = places(ids_ref[...])
-    wide = spread(place)
-    which = iota((EXPERTS * ROWS, TOK), 0) % ROWS
-    pick = jnp.where(wide == which.astype(F32), 1.0, 0.0).astype(BF16)
-    ninth = jnp.where(place == float(ROWS), 1.0, 0.0).astype(BF16)
     for c in range(ROWS):
         piece = normed_s[:, c * FOLD : (c + 1) * FOLD]
-        o_ref[:, c * FOLD : (c + 1) * FOLD] = dot(pick, piece).astype(BF16)
-        put_fold(fold_s, c, dot(ninth, piece))
+        o_ref[:, c * FOLD : (c + 1) * FOLD] = dot(pick_ref[...], piece).astype(BF16)
+        put_fold(fold_s, c, dot(nine_ref[...], piece))
     o_ref[:, D:] = whole_fold(fold_s)
 
 
@@ -198,22 +226,6 @@
     for c in range(ROWS):
         put_fold(fold_s, c, last[:, c * FOLD : (c + 1) * FOLD])
     o_ref[:, D:] = whole_fold(fold_s)
-
-
-def share_kernel(ids_ref, weights_ref, share_ref, ninth_ref):
-    def halves(value, ref):
-        high = value.astype(BF16)
-        ref[:TOK, :] = high
-        ref[TOK:, :] = (value - high.astype(F32)).astype(BF16)
-
-    ids = ids_ref[...]
-    place = places(ids)
-    weight = jnp.zeros((EXPERTS, TOK), F32)
-    for j, match in enumerate(named(ids)):
-        weight += jnp.where(match, weights_ref[j : j + 1, :], 0.0)
-    which = (iota((EXPERTS * ROWS, TOK), 0) % ROWS).astype(F32)
-    halves(jnp.where(spread(place) == which, spread(weight), 0.0).T, share_ref)
-    halves(jnp.where(place == float(ROWS), weight, 0.0).T, ninth_ref)
 
 
 def combine_kernel(y_ref, share_ref, ninth_ref, hidden_ref, o_ref, fold_s):
@@ -260,10 +272,6 @@
     line = call(functools.partial(join_kernel, parts), shaped(parts * 2 * TOK, HEAD))(*kvs)
     flipped = across(line, 2)
     gathered = [line, across(line, 1), flipped, across(flipped, 1)]
-    share, ninth = call(
-        share_kernel, (shaped(2 * TOK, EXPERTS * ROWS), shaped(2 * TOK, EXPERTS))
-    )(ids, route_weights[0].T)
-    gathered, share, ninth = lax.optimization_barrier((gathered, share, ninth))
     *attended, weight = call(
         functools.partial(attention_kernel, parts, shared),
         (query,) * parts + (shaped(*out_weight.shape),),
@@ -274,12 +282,22 @@
         in_specs=[VMEM] * (4 + parts) + [pl.BlockSpec(memory_space=pltpu.HBM)],
         out_specs=(VMEM,) * (parts + 1),
     )(*gathered, *asked, out_weight)
-    attended = [attended[0]] + [ahead(attended[s], s) for s in range(1, parts)]
+    answers = [ahead(attended[s], s) for s in range(1, parts)]
+    part, pick, nine, share, ninth = call(
+        functools.partial(prepare_kernel, parts, shared),
+        (
+            shaped(TOK, D, dtype=F32),
+            shaped(EXPERTS * ROWS, TOK),
+            shaped(EXPERTS, TOK),
+            shaped(2 * TOK, EXPERTS * ROWS),
+            shaped(2 * TOK, EXPERTS),
+        ),
+    )(attended[0], weight, ids, route_weights[0].T)
     hidden, outgoing = call(
         functools.partial(project_kernel, parts, shared),
         (shaped(TOK, D, dtype=F32), shaped(EXPERTS * ROWS, WIDE)),
         [pltpu.VMEM((TOK, D), BF16), pltpu.VMEM((FOLD // HEAD, EXPERTS * ROWS, HEAD), F32)],
-    )(*attended, weight, norm_gain[None], ids)
+    )(*answers, part, weight, norm_gain[None], pick, nine)
     arrived = exchange(outgoing, ("grp", "seq"))
     fold = pltpu.VMEM((FOLD // HEAD, EXPERTS * ROWS, HEAD), F32)
     result = call(

time: 194 us -> 194 us (level)
  no operation moved by 1% of the time
where the time goes in v1:
time: 194 us; the launch traced here: 192 us
  blocking collectives  133 us (69%)
  Pallas kernels  25.2 us (13%)
  waiting for transfers between devices  18.9 us (10%)
  starting transfers between devices  14.9 us (8%)
    all_to_all x2, blocking collectives, exchange(): return lax.all_to_all(value, axes, split_axis=0, concat_axis=0, tiled=True)  133 us
    ppermute x9, waiting for transfers between devices, ahead(): lax.ppermute(value, 'seq', [(i, (i + s * parts) % size) for i in range(si...  14 us
    ppermute x9, starting transfers between devices, ahead(): lax.ppermute(value, 'seq', [(i, (i + s * parts) % size) for i in range(si...  12.9 us
    pallas_call x1, Pallas kernels, on_device(): call(functools.partial(expert_kernel, EXPERTS), shaped(EXPERTS * ROWS, WI...  11.3 us
    pallas_call x1, Pallas kernels, on_device(): call(functools.partial(attention_kernel, parts, shared), (query,) * parts...  5.92 us
    ppermute x3, waiting for transfers between devices, across(): return lax.ppermute(value, 'seq', [(i, i ^ d) for i in range(size)])  4.88 us
  transfers between devices with their start and end apart: 12, of which 10 were waited for; matrix products, arithmetic and copies ran while one was open for 0% of the time, Pallas kernels for 0%

profile of v1, /device:TPU:4, one launch (start us, length us, event | category | flops | bytes accessed | tf_op | source)
XLA Modules:
  0.0 192.3 jit_solution(7516223427862147272)
XLA Ops:
  0.0 2.1 %shard_map.91 = (bf16[256,128]{1,0:T(8,128)(2,1)S(1)}, bf16[256,128]{1,0:T(8,128)(2,1)S(1)}, bf16[256,128]{1,0:T(8,128)(2,1)S(1)}, bf16[256,128]{1,0:T(8,128)(2,...) custom-call(bf16[128,2048]{1,0:T(8,128)(2,1)} %bitcast.28, ...), custom_call_target="tpu_custom_call" | custom-call | tf_op jit(solution)/shard_map/pallas_call | solution.py:263
  2.1 1.3 collective-permute-start
  3.3 0.8 collective-permute-start.1
  4.1 1.0 collective-permute-start.2
  5.2 1.2 collective-permute-done.refs_1_
  6.4 2.7 %collective-permute-done.1.refs_2_ = bf16[256,128]{1,0:T(8,128)(2,1)S(1)} collective-permute-done((bf16[256,128]{1,0:T(8,128)(2,1)S(1)}, bf16[256,128]{1,0:T(8,128)(2,1)S(1)}, u32[]{:S(2)}, u32[]{:S(2)}) %collective-permute-start.1) | collective-permute-done | bytes 65568 | tf_op jit(solution)/shard_map/ppermute | solution.py:257
  9.1 0.1 collective-permute-done.2.refs_3_
  9.2 2.0 %collective-permute-start.4 = (bf16[1024,128]{1,0:T(8,128)(2,1)S(1)}, bf16[1024,128]{1,0:T(8,128)(2,1)S(1)}, u32[]{:S(2)}, u32[]{:S(2)}) collective-permute-start(bf16[1024,128]{1,0:T(8,128)(2,1)S(1)} %shard_map.92.refs_0_), channel_id=1, source_target_pairs={{0,2},{1,3},{2,0},{3,1},{4,6},{5,7},{6,4},{7,5},{8,10},{9,11},{10,... | collective-permute-start | bytes 786440 | tf_op jit(solution)/shard_map/ppermute | solution.py:260
  11.2 0.0 collective-permute-start.3
  11.2 4.9 %collective-permute-done.4.refs_2_ = bf16[1024,128]{1,0:T(8,128)(2,1)S(1)} collective-permute-done((bf16[1024,128]{1,0:T(8,128)(2,1)S(1)}, bf16[1024,128]{1,0:T(8,128)(2,1)S(1)}, u32[]{:S(2)}, u32[]{:S(2)}) %collective-permute-start.4) | collective-permute-done | bytes 262176 | tf_op jit(solution)/shard_map/ppermute | solution.py:260
  16.1 0.0 collective-permute-start.5
  16.1 2.5 %collective-permute-start.6 = (bf16[512,128]{1,0:T(8,128)(2,1)}, bf16[512,128]{1,0:T(8,128)(2,1)S(1)}, u32[]{:S(2)}, u32[]{:S(2)}) collective-permute-start(bf16[512,128]{1,0:T(8,128)(2,1)} %get-tuple-element.30), channel_id=1, source_target_pairs={{0,4},{1,5},{2,6},{3,7},{4,8},{5,9},{6,10},{7,11},{8,12},{9,13},{1... | collective-permute-start | bytes 393224 | tf_op jit(solution)/shard_map/ppermute | solution.py:257
  18.6 0.0 collective-permute-start.7
  18.6 2.3 %collective-permute-start.8 = (bf16[512,128]{1,0:T(8,128)(2,1)}, bf16[512,128]{1,0:T(8,128)(2,1)S(1)}, u32[]{:S(2)}, u32[]{:S(2)}) collective-permute-start(bf16[512,128]{1,0:T(8,128)(2,1)} %get-tuple-element.32), channel_id=1, source_target_pairs={{0,12},{1,13},{2,14},{3,15},{4,0},{5,1},{6,2},{7,3},{8,4},{9,5},{1... | collective-permute-start | bytes 393224 | tf_op jit(solution)/shard_map/ppermute | solution.py:257
  20.9 1.9 collective-permute-done.6.refs_5_
  22.8 3.1 %collective-permute-done.7.refs_6_ = bf16[512,128]{1,0:T(8,128)(2,1)S(1)} collective-permute-done((bf16[512,128]{1,0:T(8,128)(2,1)}, bf16[512,128]{1,0:T(8,128)(2,1)S(1)}, u32[]{:S(2)}, u32[]{:S(2)}) %collective-permute-start.7) | collective-permute-done | bytes 131104 | tf_op jit(solution)/shard_map/ppermute | solution.py:257
  26.0 0.8 collective-permute-done.8.refs_7_
  26.8 0.0 collective-permute-done.3.refs_1_
  26.8 0.0 collective-permute-done.5.refs_3_
  26.8 0.0 copy-start.2
  26.8 0.0 copy-start.3
  26.8 5.9 %shard_map.93 = (bf16[512,128]{1,0:T(8,128)(2,1)S(1)}, bf16[512,128]{1,0:T(8,128)(2,1)S(1)}, bf16[512,128]{1,0:T(8,128)(2,1)S(1)}, bf16[512,128]{1,0:T(8,128)(2,1)S(1)}, bf16[2048,2048]{1,0:T(8,128)(2,1)S(1)}) custom-call(bf16[1024,128]{1,0:T(8,128)(2,1)S(1)} %shard_map.92.refs_0_, bf16[1024,128]{1,0:T(8,128)(2,1)S(1)} %collective-permute-done.3.refs_1_, ...), custom_call_target="tpu_custom_call" | custom-call | tf_op jit(solution)/shard_map/pallas_call | solution.py:275
  32.8 0.0 copy-start.1
  32.8 2.9 %collective-permute-start.9 = (bf16[512,128]{1,0:T(8,128)(2,1)S(1)}, bf16[512,128]{1,0:T(8,128)(2,1)S(1)}, u32[]{:S(2)}, u32[]{:S(2)}) collective-permute-start(bf16[512,128]{1,0:T(8,128)(2,1)S(1)} %get-tuple-element.33), channel_id=1, source_target_pairs={{0,4},{1,5},{2,6},{3,7},{4,8},{5,9},{6,10},{7,11},{8,12},{9,13},{1... | collective-permute-start | bytes 393224 | tf_op jit(solution)/shard_map/ppermute | solution.py:257
  35.7 0.1 collective-permute-start.10
  35.8 1.9 %collective-permute-start.11 = (bf16[512,128]{1,0:T(8,128)(2,1)S(1)}, bf16[512,128]{1,0:T(8,128)(2,1)S(1)}, u32[]{:S(2)}, u32[]{:S(2)}) collective-permute-start(bf16[512,128]{1,0:T(8,128)(2,1)S(1)} %get-tuple-element.35), channel_id=1, source_target_pairs={{0,12},{1,13},{2,14},{3,15},{4,0},{5,1},{6,2},{7,3},{8,4},{9,5},{1... | collective-permute-start | bytes 393224 | tf_op jit(solution)/shard_map/ppermute | solution.py:257
  37.7 0.0 copy-done.2
  37.7 0.0 copy-done.3
  37.7 0.0 slice-start
  37.7 0.8 shard_map.94
  38.5 1.1 collective-permute-done.9.refs_0_
  39.6 2.8 %collective-permute-done.10.refs_1_ = bf16[512,128]{1,0:T(8,128)(2,1)S(1)} collective-permute-done((bf16[512,128]{1,0:T(8,128)(2,1)S(1)}, bf16[512,128]{1,0:T(8,128)(2,1)S(1)}, u32[]{:S(2)}, u32[]{:S(2)}) %collective-permute-start.10) | collective-permute-done | bytes 131104 | tf_op jit(solution)/shard_map/ppermute | solution.py:257
  42.4 0.3 collective-permute-done.11.refs_2_
  42.7 0.0 copy-done.1
  42.7 0.0 slice-start.1
  42.7 2.6 %shard_map.95 = (f32[128,2048]{1,0:T(8,128)S(1)}, bf16[1024,2304]{1,0:T(8,128)(2,1)S(1)}) custom-call(bf16[512,128]{1,0:T(8,128)(2,1)S(1)} %collective-permute-done.9.refs_0_, bf16[512,128]{1,0:T(8,128)(2,1)S(1)} %collective-permute-done.10.refs_1_, bf16[512,128]{1,0:T(8,128)(2,1)S(1)} %collective-permute-done.11.refs_2_, ...), custom_call_target="tpu_custom_call" | custom-call | tf_op jit(solution)/shard_map/pallas_call | solution.py:296
  45.3 0.0 copy-start
  45.3 69.9 %all_to_all.22 = bf16[128,8,2304]{2,1,0:T(8,128)(2,1)S(1)} all-to-all(bf16[128,8,2304]{2,1,0:T(8,128)(2,1)S(1)} %bitcast.23), channel_id=1, replica_groups=mesh['grp'=8,'seq'=16] {'grp','seq'}, dimensions={0} | all-to-all | bytes 9437184 | tf_op jit(solution)/shard_map/all_to_all | solution.py:241
  115.2 0.0 slice-done
  115.2 0.0 slice-done.1
  115.2 0.0 copy-done
  115.3 11.3 %shard_map.96 = bf16[1024,2304]{1,0:T(8,128)(2,1)S(1)} custom-call(bf16[1024,2304]{1,0:T(8,128)(2,1)S(1)} %bitcast.18, bf16[2048,1536]{1,0:T(8,128)(2,1)S(1)} %bitcast.22, bf16[768,2048]{1,0:T(8,128)(2,1)S(1)} %bitcast.24), custom_call_target="tpu_custom_call" | custom-call | tf_op jit(solution)/shard_map/pallas_call | solution.py:303
  126.6 63.3 %all_to_all.23 = bf16[128,8,2304]{2,1,0:T(8,128)(2,1)S(1)} all-to-all(bf16[128,8,2304]{2,1,0:T(8,128)(2,1)S(1)} %bitcast.19), channel_id=1, replica_groups=mesh['grp'=8,'seq'=16] {'grp','seq'}, dimensions={0} | all-to-all | bytes 9437184 | tf_op jit(solution)/shard_map/all_to_all | solution.py:241
  189.9 2.4 %shard_map.97 = bf16[128,2048]{1,0:T(8,128)(2,1)} custom-call(bf16[1024,2304]{1,0:T(8,128)(2,1)S(1)} %bitcast.17, bf16[256,1024]{1,0:T(8,128)(2,1)S(1)} %get-tuple-element.42.share_ref, bf16[256,128]{1,0:T(8,128)(2,1)S(1)} %get-tuple-element.43.ninth_ref, f32[128,2048]{1,0:T(8,128)S(1)} %get-tuple-element.44.hidden_ref), custom_call_target="tpu_custom_call" | custom-call | tf_op jit(solution)/shard_map/pallas_call | solution.py:309
  (2 shorter events, 0.0 us)
Async XLA Ops:
  2.1 4.3 %collective-permute-start = (bf16[256,128]{1,0:T(8,128)(2,1)S(1)}, bf16[256,128]{1,0:T(8,128)(2,1)S(1)}, u32[]{:S(2)}, u32[]{:S(2)}) collective-permute-start(bf16[256,128]{1,0:T(8,128)(2,1)S(1)} %get-tuple-element.26), channel_id=1, source_target_pairs={{0,4},{1,5},{2,6},{3,7},{4,8},{5,9},{6,10},{7,11},{8,12},{9,13},{1... | collective-permute-start | bytes 196616 | tf_op jit(solution)/shard_map/ppermute | solution.py:257
  3.3 5.8 %collective-permute-start.1 = (bf16[256,128]{1,0:T(8,128)(2,1)S(1)}, bf16[256,128]{1,0:T(8,128)(2,1)S(1)}, u32[]{:S(2)}, u32[]{:S(2)}) collective-permute-start(bf16[256,128]{1,0:T(8,128)(2,1)S(1)} %get-tuple-element.27), channel_id=1, source_target_pairs={{0,8},{1,9},{2,10},{3,11},{4,12},{5,13},{6,14},{7,15},{8,0},{9,1},... | collective-permute-start | bytes 196616 | tf_op jit(solution)/shard_map/ppermute | solution.py:257
  4.1 5.0 %collective-permute-start.2 = (bf16[256,128]{1,0:T(8,128)(2,1)S(1)}, bf16[256,128]{1,0:T(8,128)(2,1)S(1)}, u32[]{:S(2)}, u32[]{:S(2)}) collective-permute-start(bf16[256,128]{1,0:T(8,128)(2,1)S(1)} %get-tuple-element.28), channel_id=1, source_target_pairs={{0,12},{1,13},{2,14},{3,15},{4,0},{5,1},{6,2},{7,3},{8,4},{9,5},{1... | collective-permute-start | bytes 196616 | tf_op jit(solution)/shard_map/ppermute | solution.py:257
  9.2 6.9 %collective-permute-start.4 = (bf16[1024,128]{1,0:T(8,128)(2,1)S(1)}, bf16[1024,128]{1,0:T(8,128)(2,1)S(1)}, u32[]{:S(2)}, u32[]{:S(2)}) collective-permute-start(bf16[1024,128]{1,0:T(8,128)(2,1)S(1)} %shard_map.92.refs_0_), channel_id=1, source_target_pairs={{0,2},{1,3},{2,0},{3,1},{4,6},{5,7},{6,4},{7,5},{8,10},{9,11},{10,... | collective-permute-start | bytes 786440 | tf_op jit(solution)/shard_map/ppermute | solution.py:260
  11.2 15.6 %collective-permute-start.3 = (bf16[1024,128]{1,0:T(8,128)(2,1)S(1)}, bf16[1024,128]{1,0:T(8,128)(2,1)S(1)}, u32[]{:S(2)}, u32[]{:S(2)}) collective-permute-start(bf16[1024,128]{1,0:T(8,128)(2,1)S(1)} %shard_map.92.refs_0_), channel_id=1, source_target_pairs={{0,1},{1,0},{2,3},{3,2},{4,5},{5,4},{6,7},{7,6},{8,9},{9,8},{10,11... | collective-permute-start | bytes 786440 | tf_op jit(solution)/shard_map/ppermute | solution.py:260
  16.1 10.7 %collective-permute-start.5 = (bf16[1024,128]{1,0:T(8,128)(2,1)S(1)}, bf16[1024,128]{1,0:T(8,128)(2,1)S(1)}, u32[]{:S(2)}, u32[]{:S(2)}) collective-permute-start(bf16[1024,128]{1,0:T(8,128)(2,1)S(1)} %collective-permute-done.4.refs_2_), channel_id=1, source_target_pairs={{0,1},{1,0},{2,3},{3,2},{4,5},{5,4},{6,7},{7,6},{8,9},{9,8},{10,11... | collective-permute-start | bytes 786440 | tf_op jit(solution)/shard_map/ppermute | solution.py:260
  16.1 6.7 %collective-permute-start.6 = (bf16[512,128]{1,0:T(8,128)(2,1)}, bf16[512,128]{1,0:T(8,128)(2,1)S(1)}, u32[]{:S(2)}, u32[]{:S(2)}) collective-permute-start(bf16[512,128]{1,0:T(8,128)(2,1)} %get-tuple-element.30), channel_id=1, source_target_pairs={{0,4},{1,5},{2,6},{3,7},{4,8},{5,9},{6,10},{7,11},{8,12},{9,13},{1... | collective-permute-start | bytes 393224 | tf_op jit(solution)/shard_map/ppermute | solution.py:257
  18.6 7.3 %collective-permute-start.7 = (bf16[512,128]{1,0:T(8,128)(2,1)}, bf16[512,128]{1,0:T(8,128)(2,1)S(1)}, u32[]{:S(2)}, u32[]{:S(2)}) collective-permute-start(bf16[512,128]{1,0:T(8,128)(2,1)} %get-tuple-element.31), channel_id=1, source_target_pairs={{0,8},{1,9},{2,10},{3,11},{4,12},{5,13},{6,14},{7,15},{8,0},{9,1},... | collective-permute-start | bytes 393224 | tf_op jit(solution)/shard_map/ppermute | solution.py:257
  18.6 8.2 %collective-permute-start.8 = (bf16[512,128]{1,0:T(8,128)(2,1)}, bf16[512,128]{1,0:T(8,128)(2,1)S(1)}, u32[]{:S(2)}, u32[]{:S(2)}) collective-permute-start(bf16[512,128]{1,0:T(8,128)(2,1)} %get-tuple-element.32), channel_id=1, source_target_pairs={{0,12},{1,13},{2,14},{3,15},{4,0},{5,1},{6,2},{7,3},{8,4},{9,5},{1... | collective-permute-start | bytes 393224 | tf_op jit(solution)/shard_map/ppermute | solution.py:257
  26.8 10.9 %copy-start.2 = (s32[1,128,8]{1,2,0:T(8,128)S(1)}, s32[1,128,8]{1,2,0:T(8,128)}, u32[]{:S(2)}) copy-start(s32[1,128,8]{1,2,0:T(8,128)} %param.12) | copy-start | bytes 12292
  26.8 10.9 %copy-start.3 = (f32[1,128,8]{1,2,0:T(8,128)S(1)}, f32[1,128,8]{1,2,0:T(8,128)}, u32[]{:S(2)}) copy-start(f32[1,128,8]{1,2,0:T(8,128)} %param.13) | copy-start | bytes 12292
  32.8 9.9 %copy-start.1 = (f32[2048]{0:T(1024)S(1)}, f32[2048]{0:T(1024)}, u32[]{:S(2)}) copy-start(f32[2048]{0:T(1024)} %param.15) | copy-start | bytes 24580
  32.8 6.8 %collective-permute-start.9 = (bf16[512,128]{1,0:T(8,128)(2,1)S(1)}, bf16[512,128]{1,0:T(8,128)(2,1)S(1)}, u32[]{:S(2)}, u32[]{:S(2)}) collective-permute-start(bf16[512,128]{1,0:T(8,128)(2,1)S(1)} %get-tuple-element.33), channel_id=1, source_target_pairs={{0,4},{1,5},{2,6},{3,7},{4,8},{5,9},{6,10},{7,11},{8,12},{9,13},{1... | collective-permute-start | bytes 393224 | tf_op jit(solution)/shard_map/ppermute | solution.py:257
  35.7 6.7 %collective-permute-start.10 = (bf16[512,128]{1,0:T(8,128)(2,1)S(1)}, bf16[512,128]{1,0:T(8,128)(2,1)S(1)}, u32[]{:S(2)}, u32[]{:S(2)}) collective-permute-start(bf16[512,128]{1,0:T(8,128)(2,1)S(1)} %get-tuple-element.34), channel_id=1, source_target_pairs={{0,8},{1,9},{2,10},{3,11},{4,12},{5,13},{6,14},{7,15},{8,0},{9,1},... | collective-permute-start | bytes 393224 | tf_op jit(solution)/shard_map/ppermute | solution.py:257
  35.8 6.9 %collective-permute-start.11 = (bf16[512,128]{1,0:T(8,128)(2,1)S(1)}, bf16[512,128]{1,0:T(8,128)(2,1)S(1)}, u32[]{:S(2)}, u32[]{:S(2)}) collective-permute-start(bf16[512,128]{1,0:T(8,128)(2,1)S(1)} %get-tuple-element.35), channel_id=1, source_target_pairs={{0,12},{1,13},{2,14},{3,15},{4,0},{5,1},{6,2},{7,3},{8,4},{9,5},{1... | collective-permute-start | bytes 393224 | tf_op jit(solution)/shard_map/ppermute | solution.py:257
  37.7 77.5 %slice-start = ((s8[6291456]{0:T(1024)(128)(4,1)}), s8[4194304]{0:T(1024)(128)(4,1)S(1)}, s32[]{:S(2)}) async-start(s8[6291456]{0:T(1024)(128)(4,1)} %bitcast.20), calls=%async_computation.2 | async-start | bytes 8388608
  42.7 72.6 %slice-start.1 = ((s8[6291456]{0:T(1024)(128)(4,1)}), s8[2097152]{0:T(1024)(128)(4,1)S(1)}, s32[]{:S(2)}) async-start(s8[6291456]{0:T(1024)(128)(4,1)} %bitcast.20), calls=%async_computation.3 | async-start | bytes 4194304
  45.3 70.0 %copy-start = (bf16[1,768,2048]{2,1,0:T(8,128)(2,1)S(1)}, bf16[1,768,2048]{2,1,0:T(8,128)(2,1)}, u32[]{:S(2)}) copy-start(bf16[1,768,2048]{2,1,0:T(8,128)(2,1)} %param.17) | copy-start | bytes 9437188

commit v2 on v1

--- a/solution.py
+++ b/solution.py
@@ -268,10 +268,12 @@
         in_specs=[pl.BlockSpec(memory_space=pltpu.HBM)] * 3,
     )(queries[0], keys[0], values[0])
     kvs = [sent[0]] + [ahead(sent[s], s) for s in range(1, parts)]
-    asked = [sent[parts]] + [ahead(sent[parts + s], s) for s in range(1, parts)]
+    asked = [sent[parts]] + [ahead(sent[parts + s], s) for s in range(1, parts - 1)]
     line = call(functools.partial(join_kernel, parts), shaped(parts * 2 * TOK, HEAD))(*kvs)
     flipped = across(line, 2)
-    gathered = [line, across(line, 1), flipped, across(flipped, 1)]
+    asked.append(ahead(sent[2 * parts - 1], parts - 1))
+    opposite = across(flipped, 1)
+    gathered = [line, across(line, 1), flipped, opposite]
     *attended, weight = call(
         functools.partial(attention_kernel, parts, shared),
         (query,) * parts + (shaped(*out_weight.shape),),

time: 194 us -> 194 us (level)
  no operation moved by 1% of the time
where the time goes in v2:
time: 194 us; the launch traced here: 192 us
  blocking collectives  133 us (69%)
  Pallas kernels  25.2 us (13%)
  waiting for transfers between devices  18.9 us (10%)
  starting transfers between devices  14.9 us (8%)
    all_to_all x2, blocking collectives, exchange(): return lax.all_to_all(value, axes, split_axis=0, concat_axis=0, tiled=True)  133 us
    ppermute x9, waiting for transfers between devices, ahead(): lax.ppermute(value, 'seq', [(i, (i + s * parts) % size) for i in range(si...  14 us
    ppermute x9, starting transfers between devices, ahead(): lax.ppermute(value, 'seq', [(i, (i + s * parts) % size) for i in range(si...  12.9 us
    pallas_call x1, Pallas kernels, on_device(): call(functools.partial(expert_kernel, EXPERTS), shaped(EXPERTS * ROWS, WI...  11.3 us
    pallas_call x1, Pallas kernels, on_device(): call(functools.partial(attention_kernel, parts, shared), (query,) * parts...  5.92 us
    ppermute x3, waiting for transfers between devices, across(): return lax.ppermute(value, 'seq', [(i, i ^ d) for i in range(size)])  4.88 us
  transfers between devices with their start and end apart: 12, of which 10 were waited for; matrix products, arithmetic and copies ran while one was open for 0% of the time, Pallas kernels for 0%

profile of v2, /device:TPU:4, one launch (start us, length us, event | category | flops | bytes accessed | tf_op | source)
XLA Modules:
  0.0 192.3 jit_solution(7516223427862147272)
XLA Ops:
  0.0 2.1 %shard_map.91 = (bf16[256,128]{1,0:T(8,128)(2,1)S(1)}, bf16[256,128]{1,0:T(8,128)(2,1)S(1)}, bf16[256,128]{1,0:T(8,128)(2,1)S(1)}, bf16[256,128]{1,0:T(8,128)(2,...) custom-call(bf16[128,2048]{1,0:T(8,128)(2,1)} %bitcast.28, ...), custom_call_target="tpu_custom_call" | custom-call | tf_op jit(solution)/shard_map/pallas_call | solution.py:263
  2.1 1.3 collective-permute-start
  3.3 0.8 collective-permute-start.1
  4.1 1.0 collective-permute-start.2
  5.2 1.2 collective-permute-done.refs_1_
  6.4 2.7 %collective-permute-done.1.refs_2_ = bf16[256,128]{1,0:T(8,128)(2,1)S(1)} collective-permute-done((bf16[256,128]{1,0:T(8,128)(2,1)S(1)}, bf16[256,128]{1,0:T(8,128)(2,1)S(1)}, u32[]{:S(2)}, u32[]{:S(2)}) %collective-permute-start.1) | collective-permute-done | bytes 65568 | tf_op jit(solution)/shard_map/ppermute | solution.py:257
  9.1 0.1 collective-permute-done.2.refs_3_
  9.2 2.0 %collective-permute-start.4 = (bf16[1024,128]{1,0:T(8,128)(2,1)S(1)}, bf16[1024,128]{1,0:T(8,128)(2,1)S(1)}, u32[]{:S(2)}, u32[]{:S(2)}) collective-permute-start(bf16[1024,128]{1,0:T(8,128)(2,1)S(1)} %shard_map.92.refs_0_), channel_id=1, source_target_pairs={{0,2},{1,3},{2,0},{3,1},{4,6},{5,7},{6,4},{7,5},{8,10},{9,11},{10,... | collective-permute-start | bytes 786440 | tf_op jit(solution)/shard_map/ppermute | solution.py:260
  11.2 0.0 collective-permute-start.3
  11.2 4.9 %collective-permute-done.4.refs_2_ = bf16[1024,128]{1,0:T(8,128)(2,1)S(1)} collective-permute-done((bf16[1024,128]{1,0:T(8,128)(2,1)S(1)}, bf16[1024,128]{1,0:T(8,128)(2,1)S(1)}, u32[]{:S(2)}, u32[]{:S(2)}) %collective-permute-start.4) | collective-permute-done | bytes 262176 | tf_op jit(solution)/shard_map/ppermute | solution.py:260
  16.1 0.0 collective-permute-start.5
  16.1 2.5 %collective-permute-start.6 = (bf16[512,128]{1,0:T(8,128)(2,1)}, bf16[512,128]{1,0:T(8,128)(2,1)S(1)}, u32[]{:S(2)}, u32[]{:S(2)}) collective-permute-start(bf16[512,128]{1,0:T(8,128)(2,1)} %get-tuple-element.30), channel_id=1, source_target_pairs={{0,4},{1,5},{2,6},{3,7},{4,8},{5,9},{6,10},{7,11},{8,12},{9,13},{1... | collective-permute-start | bytes 393224 | tf_op jit(solution)/shard_map/ppermute | solution.py:257
  18.6 0.0 collective-permute-start.7
  18.6 2.3 %collective-permute-start.8 = (bf16[512,128]{1,0:T(8,128)(2,1)}, bf16[512,128]{1,0:T(8,128)(2,1)S(1)}, u32[]{:S(2)}, u32[]{:S(2)}) collective-permute-start(bf16[512,128]{1,0:T(8,128)(2,1)} %get-tuple-element.32), channel_id=1, source_target_pairs={{0,12},{1,13},{2,14},{3,15},{4,0},{5,1},{6,2},{7,3},{8,4},{9,5},{1... | collective-permute-start | bytes 393224 | tf_op jit(solution)/shard_map/ppermute | solution.py:257
  20.9 1.9 collective-permute-done.6.refs_5_
  22.8 3.1 %collective-permute-done.7.refs_6_ = bf16[512,128]{1,0:T(8,128)(2,1)S(1)} collective-permute-done((bf16[512,128]{1,0:T(8,128)(2,1)}, bf16[512,128]{1,0:T(8,128)(2,1)S(1)}, u32[]{:S(2)}, u32[]{:S(2)}) %collective-permute-start.7) | collective-permute-done | bytes 131104 | tf_op jit(solution)/shard_map/ppermute | solution.py:257
  26.0 0.8 collective-permute-done.8.refs_7_
  26.8 0.0 collective-permute-done.3.refs_1_
  26.8 0.0 collective-permute-done.5.refs_3_
  26.8 0.0 copy-start.2
  26.8 0.0 copy-start.3
  26.8 5.9 %shard_map.93 = (bf16[512,128]{1,0:T(8,128)(2,1)S(1)}, bf16[512,128]{1,0:T(8,128)(2,1)S(1)}, bf16[512,128]{1,0:T(8,128)(2,1)S(1)}, bf16[512,128]{1,0:T(8,128)(2,1)S(1)}, bf16[2048,2048]{1,0:T(8,128)(2,1)S(1)}) custom-call(bf16[1024,128]{1,0:T(8,128)(2,1)S(1)} %shard_map.92.refs_0_, bf16[1024,128]{1,0:T(8,128)(2,1)S(1)} %collective-permute-done.3.refs_1_, ...), custom_call_target="tpu_custom_call" | custom-call | tf_op jit(solution)/shard_map/pallas_call | solution.py:277
  32.8 0.0 copy-start.1
  32.8 2.9 %collective-permute-start.9 = (bf16[512,128]{1,0:T(8,128)(2,1)S(1)}, bf16[512,128]{1,0:T(8,128)(2,1)S(1)}, u32[]{:S(2)}, u32[]{:S(2)}) collective-permute-start(bf16[512,128]{1,0:T(8,128)(2,1)S(1)} %get-tuple-element.33), channel_id=1, source_target_pairs={{0,4},{1,5},{2,6},{3,7},{4,8},{5,9},{6,10},{7,11},{8,12},{9,13},{1... | collective-permute-start | bytes 393224 | tf_op jit(solution)/shard_map/ppermute | solution.py:257
  35.7 0.1 collective-permute-start.10
  35.8 1.9 %collective-permute-start.11 = (bf16[512,128]{1,0:T(8,128)(2,1)S(1)}, bf16[512,128]{1,0:T(8,128)(2,1)S(1)}, u32[]{:S(2)}, u32[]{:S(2)}) collective-permute-start(bf16[512,128]{1,0:T(8,128)(2,1)S(1)} %get-tuple-element.35), channel_id=1, source_target_pairs={{0,12},{1,13},{2,14},{3,15},{4,0},{5,1},{6,2},{7,3},{8,4},{9,5},{1... | collective-permute-start | bytes 393224 | tf_op jit(solution)/shard_map/ppermute | solution.py:257
  37.7 0.0 copy-done.2
  37.7 0.0 copy-done.3
  37.7 0.0 slice-start
  37.7 0.8 shard_map.94
  38.5 1.1 collective-permute-done.9.refs_0_
  39.6 2.8 %collective-permute-done.10.refs_1_ = bf16[512,128]{1,0:T(8,128)(2,1)S(1)} collective-permute-done((bf16[512,128]{1,0:T(8,128)(2,1)S(1)}, bf16[512,128]{1,0:T(8,128)(2,1)S(1)}, u32[]{:S(2)}, u32[]{:S(2)}) %collective-permute-start.10) | collective-permute-done | bytes 131104 | tf_op jit(solution)/shard_map/ppermute | solution.py:257
  42.4 0.3 collective-permute-done.11.refs_2_
  42.7 0.0 copy-done.1
  42.7 0.0 slice-start.1
  42.7 2.6 %shard_map.95 = (f32[128,2048]{1,0:T(8,128)S(1)}, bf16[1024,2304]{1,0:T(8,128)(2,1)S(1)}) custom-call(bf16[512,128]{1,0:T(8,128)(2,1)S(1)} %collective-permute-done.9.refs_0_, bf16[512,128]{1,0:T(8,128)(2,1)S(1)} %collective-permute-done.10.refs_1_, bf16[512,128]{1,0:T(8,128)(2,1)S(1)} %collective-permute-done.11.refs_2_, ...), custom_call_target="tpu_custom_call" | custom-call | tf_op jit(solution)/shard_map/pallas_call | solution.py:298
  45.3 0.0 copy-start
  45.3 69.9 %all_to_all.22 = bf16[128,8,2304]{2,1,0:T(8,128)(2,1)S(1)} all-to-all(bf16[128,8,2304]{2,1,0:T(8,128)(2,1)S(1)} %bitcast.23), channel_id=1, replica_groups=mesh['grp'=8,'seq'=16] {'grp','seq'}, dimensions={0} | all-to-all | bytes 9437184 | tf_op jit(solution)/shard_map/all_to_all | solution.py:241
  115.2 0.0 slice-done
  115.2 0.0 slice-done.1
  115.2 0.0 copy-done
  115.3 11.3 %shard_map.96 = bf16[1024,2304]{1,0:T(8,128)(2,1)S(1)} custom-call(bf16[1024,2304]{1,0:T(8,128)(2,1)S(1)} %bitcast.18, bf16[2048,1536]{1,0:T(8,128)(2,1)S(1)} %bitcast.22, bf16[768,2048]{1,0:T(8,128)(2,1)S(1)} %bitcast.24), custom_call_target="tpu_custom_call" | custom-call | tf_op jit(solution)/shard_map/pallas_call | solution.py:305
  126.6 63.3 %all_to_all.23 = bf16[128,8,2304]{2,1,0:T(8,128)(2,1)S(1)} all-to-all(bf16[128,8,2304]{2,1,0:T(8,128)(2,1)S(1)} %bitcast.19), channel_id=1, replica_groups=mesh['grp'=8,'seq'=16] {'grp','seq'}, dimensions={0} | all-to-all | bytes 9437184 | tf_op jit(solution)/shard_map/all_to_all | solution.py:241
  189.9 2.4 %shard_map.97 = bf16[128,2048]{1,0:T(8,128)(2,1)} custom-call(bf16[1024,2304]{1,0:T(8,128)(2,1)S(1)} %bitcast.17, bf16[256,1024]{1,0:T(8,128)(2,1)S(1)} %get-tuple-element.42.share_ref, bf16[256,128]{1,0:T(8,128)(2,1)S(1)} %get-tuple-element.43.ninth_ref, f32[128,2048]{1,0:T(8,128)S(1)} %get-tuple-element.44.hidden_ref), custom_call_target="tpu_custom_call" | custom-call | tf_op jit(solution)/shard_map/pallas_call | solution.py:311
  (2 shorter events, 0.0 us)
Async XLA Ops:
  2.1 4.3 %collective-permute-start = (bf16[256,128]{1,0:T(8,128)(2,1)S(1)}, bf16[256,128]{1,0:T(8,128)(2,1)S(1)}, u32[]{:S(2)}, u32[]{:S(2)}) collective-permute-start(bf16[256,128]{1,0:T(8,128)(2,1)S(1)} %get-tuple-element.26), channel_id=1, source_target_pairs={{0,4},{1,5},{2,6},{3,7},{4,8},{5,9},{6,10},{7,11},{8,12},{9,13},{1... | collective-permute-start | bytes 196616 | tf_op jit(solution)/shard_map/ppermute | solution.py:257
  3.3 5.8 %collective-permute-start.1 = (bf16[256,128]{1,0:T(8,128)(2,1)S(1)}, bf16[256,128]{1,0:T(8,128)(2,1)S(1)}, u32[]{:S(2)}, u32[]{:S(2)}) collective-permute-start(bf16[256,128]{1,0:T(8,128)(2,1)S(1)} %get-tuple-element.27), channel_id=1, source_target_pairs={{0,8},{1,9},{2,10},{3,11},{4,12},{5,13},{6,14},{7,15},{8,0},{9,1},... | collective-permute-start | bytes 196616 | tf_op jit(solution)/shard_map/ppermute | solution.py:257
  4.1 5.0 %collective-permute-start.2 = (bf16[256,128]{1,0:T(8,128)(2,1)S(1)}, bf16[256,128]{1,0:T(8,128)(2,1)S(1)}, u32[]{:S(2)}, u32[]{:S(2)}) collective-permute-start(bf16[256,128]{1,0:T(8,128)(2,1)S(1)} %get-tuple-element.28), channel_id=1, source_target_pairs={{0,12},{1,13},{2,14},{3,15},{4,0},{5,1},{6,2},{7,3},{8,4},{9,5},{1... | collective-permute-start | bytes 196616 | tf_op jit(solution)/shard_map/ppermute | solution.py:257
  9.2 6.9 %collective-permute-start.4 = (bf16[1024,128]{1,0:T(8,128)(2,1)S(1)}, bf16[1024,128]{1,0:T(8,128)(2,1)S(1)}, u32[]{:S(2)}, u32[]{:S(2)}) collective-permute-start(bf16[1024,128]{1,0:T(8,128)(2,1)S(1)} %shard_map.92.refs_0_), channel_id=1, source_target_pairs={{0,2},{1,3},{2,0},{3,1},{4,6},{5,7},{6,4},{7,5},{8,10},{9,11},{10,... | collective-permute-start | bytes 786440 | tf_op jit(solution)/shard_map/ppermute | solution.py:260
  11.2 15.6 %collective-permute-start.3 = (bf16[1024,128]{1,0:T(8,128)(2,1)S(1)}, bf16[1024,128]{1,0:T(8,128)(2,1)S(1)}, u32[]{:S(2)}, u32[]{:S(2)}) collective-permute-start(bf16[1024,128]{1,0:T(8,128)(2,1)S(1)} %shard_map.92.refs_0_), channel_id=1, source_target_pairs={{0,1},{1,0},{2,3},{3,2},{4,5},{5,4},{6,7},{7,6},{8,9},{9,8},{10,11... | collective-permute-start | bytes 786440 | tf_op jit(solution)/shard_map/ppermute | solution.py:260
  16.1 10.7 %collective-permute-start.5 = (bf16[1024,128]{1,0:T(8,128)(2,1)S(1)}, bf16[1024,128]{1,0:T(8,128)(2,1)S(1)}, u32[]{:S(2)}, u32[]{:S(2)}) collective-permute-start(bf16[1024,128]{1,0:T(8,128)(2,1)S(1)} %collective-permute-done.4.refs_2_), channel_id=1, source_target_pairs={{0,1},{1,0},{2,3},{3,2},{4,5},{5,4},{6,7},{7,6},{8,9},{9,8},{10,11... | collective-permute-start | bytes 786440 | tf_op jit(solution)/shard_map/ppermute | solution.py:260
  16.1 6.7 %collective-permute-start.6 = (bf16[512,128]{1,0:T(8,128)(2,1)}, bf16[512,128]{1,0:T(8,128)(2,1)S(1)}, u32[]{:S(2)}, u32[]{:S(2)}) collective-permute-start(bf16[512,128]{1,0:T(8,128)(2,1)} %get-tuple-element.30), channel_id=1, source_target_pairs={{0,4},{1,5},{2,6},{3,7},{4,8},{5,9},{6,10},{7,11},{8,12},{9,13},{1... | collective-permute-start | bytes 393224 | tf_op jit(solution)/shard_map/ppermute | solution.py:257
  18.6 7.3 %collective-permute-start.7 = (bf16[512,128]{1,0:T(8,128)(2,1)}, bf16[512,128]{1,0:T(8,128)(2,1)S(1)}, u32[]{:S(2)}, u32[]{:S(2)}) collective-permute-start(bf16[512,128]{1,0:T(8,128)(2,1)} %get-tuple-element.31), channel_id=1, source_target_pairs={{0,8},{1,9},{2,10},{3,11},{4,12},{5,13},{6,14},{7,15},{8,0},{9,1},... | collective-permute-start | bytes 393224 | tf_op jit(solution)/shard_map/ppermute | solution.py:257
  18.6 8.2 %collective-permute-start.8 = (bf16[512,128]{1,0:T(8,128)(2,1)}, bf16[512,128]{1,0:T(8,128)(2,1)S(1)}, u32[]{:S(2)}, u32[]{:S(2)}) collective-permute-start(bf16[512,128]{1,0:T(8,128)(2,1)} %get-tuple-element.32), channel_id=1, source_target_pairs={{0,12},{1,13},{2,14},{3,15},{4,0},{5,1},{6,2},{7,3},{8,4},{9,5},{1... | collective-permute-start | bytes 393224 | tf_op jit(solution)/shard_map/ppermute | solution.py:257
  26.8 10.9 %copy-start.2 = (s32[1,128,8]{1,2,0:T(8,128)S(1)}, s32[1,128,8]{1,2,0:T(8,128)}, u32[]{:S(2)}) copy-start(s32[1,128,8]{1,2,0:T(8,128)} %param.12) | copy-start | bytes 12292
  26.8 10.9 %copy-start.3 = (f32[1,128,8]{1,2,0:T(8,128)S(1)}, f32[1,128,8]{1,2,0:T(8,128)}, u32[]{:S(2)}) copy-start(f32[1,128,8]{1,2,0:T(8,128)} %param.13) | copy-start | bytes 12292
  32.8 9.9 %copy-start.1 = (f32[2048]{0:T(1024)S(1)}, f32[2048]{0:T(1024)}, u32[]{:S(2)}) copy-start(f32[2048]{0:T(1024)} %param.15) | copy-start | bytes 24580
  32.8 6.8 %collective-permute-start.9 = (bf16[512,128]{1,0:T(8,128)(2,1)S(1)}, bf16[512,128]{1,0:T(8,128)(2,1)S(1)}, u32[]{:S(2)}, u32[]{:S(2)}) collective-permute-start(bf16[512,128]{1,0:T(8,128)(2,1)S(1)} %get-tuple-element.33), channel_id=1, source_target_pairs={{0,4},{1,5},{2,6},{3,7},{4,8},{5,9},{6,10},{7,11},{8,12},{9,13},{1... | collective-permute-start | bytes 393224 | tf_op jit(solution)/shard_map/ppermute | solution.py:257
  35.7 6.7 %collective-permute-start.10 = (bf16[512,128]{1,0:T(8,128)(2,1)S(1)}, bf16[512,128]{1,0:T(8,128)(2,1)S(1)}, u32[]{:S(2)}, u32[]{:S(2)}) collective-permute-start(bf16[512,128]{1,0:T(8,128)(2,1)S(1)} %get-tuple-element.34), channel_id=1, source_target_pairs={{0,8},{1,9},{2,10},{3,11},{4,12},{5,13},{6,14},{7,15},{8,0},{9,1},... | collective-permute-start | bytes 393224 | tf_op jit(solution)/shard_map/ppermute | solution.py:257
  35.8 6.9 %collective-permute-start.11 = (bf16[512,128]{1,0:T(8,128)(2,1)S(1)}, bf16[512,128]{1,0:T(8,128)(2,1)S(1)}, u32[]{:S(2)}, u32[]{:S(2)}) collective-permute-start(bf16[512,128]{1,0:T(8,128)(2,1)S(1)} %get-tuple-element.35), channel_id=1, source_target_pairs={{0,12},{1,13},{2,14},{3,15},{4,0},{5,1},{6,2},{7,3},{8,4},{9,5},{1... | collective-permute-start | bytes 393224 | tf_op jit(solution)/shard_map/ppermute | solution.py:257
  37.7 77.5 %slice-start = ((s8[6291456]{0:T(1024)(128)(4,1)}), s8[4194304]{0:T(1024)(128)(4,1)S(1)}, s32[]{:S(2)}) async-start(s8[6291456]{0:T(1024)(128)(4,1)} %bitcast.20), calls=%async_computation.2 | async-start | bytes 8388608
  42.7 72.6 %slice-start.1 = ((s8[6291456]{0:T(1024)(128)(4,1)}), s8[2097152]{0:T(1024)(128)(4,1)S(1)}, s32[]{:S(2)}) async-start(s8[6291456]{0:T(1024)(128)(4,1)} %bitcast.20), calls=%async_computation.3 | async-start | bytes 4194304
  45.3 70.0 %copy-start = (bf16[1,768,2048]{2,1,0:T(8,128)(2,1)S(1)}, bf16[1,768,2048]{2,1,0:T(8,128)(2,1)}, u32[]{:S(2)}) copy-start(bf16[1,768,2048]{2,1,0:T(8,128)(2,1)} %param.17) | copy-start | bytes 9437188
